TPU v7x, 32 devices: a whole 2x2x4 slice. The times are simulated.
32 devices in a mesh: section: 2 (over y), expert: 4 (over z), dp: 4 (over x, core).
Axes of the slice: x: 2, y: 2, z: 4, core: 2. Of those that a mesh axis runs over, the one named last changes fastest.
Arguments:
- residual: bfloat16 [4096, 2048], P(('section', 'expert', 'dp')), may hold values from -12 to 12
- queries: bfloat16 [4096, 1024], P(('section', 'expert', 'dp')), may hold values from -6 to 6
- attn_keys: bfloat16 [4096, 1024], P(('section', 'expert', 'dp')), may hold values from -6 to 6
- attn_values: bfloat16 [4096, 1024], P(('section', 'expert', 'dp')), may hold values from -6 to 6
- out_weight: bfloat16 [1024, 2048], P('expert'), may hold values from -0.1875 to 0.1875
- norm_gain: float32 [2048], replicated, may hold values from 0.25 to 1.75
- gate_weight: bfloat16 [4, 2048, 4096], P('expert', None, 'dp'), may hold values from -0.125 to 0.125
- up_weight: bfloat16 [4, 2048, 4096], P('expert', None, 'dp'), may hold values from -0.125 to 0.125
- down_weight: bfloat16 [4, 4096, 2048], P('expert', 'dp'), may hold values from -0.09375 to 0.09375
- expert_ids: int32 [4096, 1], P(('section', 'expert', 'dp')), may hold values from 0 to 3; in each aligned block of 128 rows (0 to 127, 128 to 255, ...) at most 64 rows name the same one
- out_grad: bfloat16 [4096, 2048], P(('section', 'expert', 'dp')), may hold values from -6 to 6
Outputs:
- layer_out: bfloat16 [4096, 2048], P(('section', 'expert', 'dp'))
- resid_grad: bfloat16 [4096, 2048], P(('section', 'expert', 'dp'))
- query_grad: bfloat16 [4096, 1024], P(('section', 'expert', 'dp'))
- key_grad: bfloat16 [4096, 1024], P(('section', 'expert', 'dp'))
- value_grad: bfloat16 [4096, 1024], P(('section', 'expert', 'dp'))
- weight_grad: float32 [1024, 2048], P('expert')
Inputs may be any that keep to these rules, and one draw needn't show every extreme that they name: `expert_ids`: no expert is named by more than 64 of the 128 rows of one device (an aligned block); in every draw some block names one expert exactly 64 times.
All inputs are finite; a program needn't handle non-finite values.
Results may differ from a plain program's by a relative error of at most 0.023.
Values may be sent and summed in bfloat16 or wider, within the bound.
A program may use at most 128 MiB of HBM per device.

v0:
```python
import math
import jax
import jax.numpy as jnp
from jax import lax
from jax.sharding import PartitionSpec as P

D = 2048
HEADS = 8
HEAD = 128
A = 1024
FF = 4096
epsilon = 1e-06


def contract_last(left_side, right_side):
    return lax.dot_general(
        left_side, right_side, (((1,), (1,)), ((), ())), preferred_element_type=jnp.float32
    )


def contract_first(left_side, right_side):
    return lax.dot_general(
        left_side, right_side, (((0,), (0,)), ((), ())), preferred_element_type=jnp.float32
    )


def shards(
    residual,
    queries,
    attn_keys,
    attn_values,
    out_weight,
    norm_gain,
    gate_weight,
    up_weight,
    down_weight,
    expert_ids,
    out_grad,
):
    tokens_here = residual.shape[0]
    experts = lax.axis_size("expert")
    data_ways = lax.axis_size("dp")
    capacity = max(tokens_here // 8, 2 * tokens_here // experts)
    inv_root = 1.0 / math.sqrt(HEAD)
    keys_all, values_all = (
        lax.all_gather(attn_keys, "dp", axis=0, tiled=True),
        lax.all_gather(attn_values, "dp", axis=0, tiled=True),
    )
    query_heads = queries.reshape(tokens_here, HEADS, HEAD)
    key_heads = keys_all.reshape(-1, HEADS, HEAD)
    value_heads = values_all.reshape(-1, HEADS, HEAD)
    scores = (
        jnp.einsum("thd,shd->hts", query_heads, key_heads, preferred_element_type=jnp.float32)
        * inv_root
    )
    row_peak = jnp.max(scores, axis=-1, keepdims=True)
    exp_scores = jnp.exp(scores - row_peak)
    attn_probs = exp_scores / jnp.sum(exp_scores, axis=-1, keepdims=True)
    probs_low = attn_probs.astype(jnp.bfloat16)
    attended = (
        jnp.einsum("hts,shd->thd", probs_low, value_heads, preferred_element_type=jnp.float32)
        .reshape(tokens_here, A)
        .astype(jnp.bfloat16)
    )
    full_out = lax.all_gather(out_weight, "expert", axis=0, tiled=True)
    hidden = residual.astype(jnp.float32) + jnp.dot(
        attended, full_out, preferred_element_type=jnp.float32
    )
    inv_rms = lax.rsqrt(jnp.mean(hidden * hidden, axis=-1, keepdims=True) + epsilon)
    unit_rows = hidden * inv_rms
    normed = (unit_rows * norm_gain).astype(jnp.bfloat16)
    expert_of = expert_ids[:, 0]
    onehot = (expert_of[:, None] == jnp.arange(experts, dtype=jnp.int32)[None, :]).astype(
        jnp.bfloat16
    )
    row_iota = jnp.arange(tokens_here, dtype=jnp.int32)
    earlier_mask = (row_iota[:, None] > row_iota[None, :]).astype(jnp.bfloat16)
    earlier = jnp.dot(earlier_mask, onehot, preferred_element_type=jnp.float32)
    rank_index = jnp.sum(earlier * onehot.astype(jnp.float32), axis=1).astype(jnp.int32)
    slot_index = expert_of * capacity + rank_index
    empty_rows = jnp.zeros((experts * capacity, D), jnp.bfloat16)
    send_buffer = empty_rows.at[slot_index].set(normed).reshape(experts, capacity, D)
    gate_local = gate_weight[0]
    up_local = up_weight[0]
    down_local = down_weight[0]
    block_width = FF // data_ways
    arrived = lax.all_to_all(send_buffer, "expert", split_axis=0, concat_axis=0, tiled=True)
    piece_rows = arrived.shape[1]
    gathered = lax.all_gather(arrived, "dp", axis=0, tiled=True)
    flattened = gathered.reshape(-1, D)
    gate_pre = jnp.dot(flattened, gate_local, preferred_element_type=jnp.float32)
    up_pre = jnp.dot(flattened, up_local, preferred_element_type=jnp.float32)
    activated = (jax.nn.silu(gate_pre) * up_pre).astype(jnp.bfloat16)
    partial_out = jnp.dot(activated, down_local, preferred_element_type=jnp.float32)
    summed = lax.psum_scatter(
        partial_out.reshape(data_ways * experts, piece_rows, D).astype(jnp.bfloat16),
        "dp",
        scatter_dimension=0,
        tiled=True,
    )
    returned = lax.all_to_all(summed, "expert", split_axis=0, concat_axis=0, tiled=True)
    gate_saved = gate_pre.reshape(data_ways * experts, piece_rows, block_width)
    up_saved = up_pre.reshape(data_ways * experts, piece_rows, block_width)
    expert_back = returned.reshape(experts * capacity, D)[slot_index]
    layer_out = (hidden + expert_back.astype(jnp.float32)).astype(jnp.bfloat16)
    grad_buffer = empty_rows.at[slot_index].set(out_grad).reshape(experts, capacity, D)
    grad_arrived = lax.all_to_all(grad_buffer, "expert", split_axis=0, concat_axis=0, tiled=True)
    grad_gathered = lax.all_gather(grad_arrived, "dp", axis=0, tiled=True)
    grad_flat = grad_gathered.reshape(-1, D)
    gate_pre = gate_saved.reshape(-1, block_width)
    up_pre = up_saved.reshape(-1, block_width)
    sigmoid_gate = jax.nn.sigmoid(gate_pre)
    grad_act = contract_last(grad_flat, down_local)
    grad_gate = (grad_act * up_pre * sigmoid_gate * (1.0 + gate_pre * (1.0 - sigmoid_gate))).astype(
        jnp.bfloat16
    )
    grad_up = (grad_act * jax.nn.silu(gate_pre)).astype(jnp.bfloat16)
    partial_grad = contract_last(grad_gate, gate_local) + contract_last(grad_up, up_local)
    grad_normed_rows = lax.psum_scatter(
        partial_grad.reshape(data_ways * experts, capacity, D).astype(jnp.bfloat16),
        "dp",
        scatter_dimension=0,
        tiled=True,
    )
    grad_returned = lax.all_to_all(
        grad_normed_rows, "expert", split_axis=0, concat_axis=0, tiled=True
    )
    grad_normed = grad_returned.reshape(experts * capacity, D)[slot_index].astype(jnp.float32)
    scaled = grad_normed * norm_gain
    resid_grad = (
        out_grad.astype(jnp.float32)
        + inv_rms * (scaled - unit_rows * jnp.mean(scaled * unit_rows, axis=-1, keepdims=True))
    ).astype(jnp.bfloat16)
    grad_shard = lax.psum_scatter(
        contract_first(attended, resid_grad).astype(jnp.bfloat16),
        "expert",
        scatter_dimension=0,
        tiled=True,
    )
    weight_grad = lax.psum(grad_shard, ("section", "dp")).astype(jnp.float32)
    grad_attended = contract_last(resid_grad, full_out).astype(jnp.bfloat16)
    grad_heads = grad_attended.reshape(tokens_here, HEADS, HEAD)
    grad_probs = jnp.einsum(
        "thd,shd->hts", grad_heads, value_heads, preferred_element_type=jnp.float32
    )
    row_delta = jnp.sum(attn_probs * grad_probs, axis=-1, keepdims=True)
    grad_scores = (attn_probs * (grad_probs - row_delta)).astype(jnp.bfloat16)
    query_grad = (
        (
            jnp.einsum("hts,shd->thd", grad_scores, key_heads, preferred_element_type=jnp.float32)
            * inv_root
        )
        .reshape(tokens_here, A)
        .astype(jnp.bfloat16)
    )
    key_part = (
        jnp.einsum("hts,thd->shd", grad_scores, query_heads, preferred_element_type=jnp.float32)
        * inv_root
    )
    value_part = jnp.einsum(
        "hts,thd->shd", probs_low, grad_heads, preferred_element_type=jnp.float32
    )
    key_value = lax.psum_scatter(
        jnp.concatenate(
            [
                key_part.reshape(lax.axis_size("dp") * tokens_here, A),
                value_part.reshape(lax.axis_size("dp") * tokens_here, A),
            ],
            axis=1,
        ).astype(jnp.bfloat16),
        "dp",
        scatter_dimension=0,
        tiled=True,
    ).astype(jnp.float32)
    key_grad = key_value[:, :A].astype(jnp.bfloat16)
    value_grad = key_value[:, A:].astype(jnp.bfloat16)
    return (layer_out, resid_grad, query_grad, key_grad, value_grad, weight_grad)


def solution(mesh):
    return jax.shard_map(
        shards,
        mesh=mesh,
        in_specs=(
            P(("section", "expert", "dp"), None),
            P(("section", "expert", "dp"), None),
            P(("section", "expert", "dp"), None),
            P(("section", "expert", "dp"), None),
            P("expert", None),
            P(),
            P("expert", None, "dp"),
            P("expert", None, "dp"),
            P("expert", "dp", None),
            P(("section", "expert", "dp"), None),
            P(("section", "expert", "dp"), None),
        ),
        out_specs=(
            P(("section", "expert", "dp"), None),
            P(("section", "expert", "dp"), None),
            P(("section", "expert", "dp"), None),
            P(("section", "expert", "dp"), None),
            P(("section", "expert", "dp"), None),
            P("expert", None),
        ),
        check_vma=False,
    )
```

profile of v0, /device:TPU:0, one launch (start us, length us, event | category | flops | bytes accessed | tf_op | source)
XLA Modules:
  0.0 544.3 jit_solution(3329325886076428349)
XLA Ops:
  7.2 0.0 all-gather.8.cloned.1.call-start
  7.2 0.7 all-gather.8.cloned.1.call-update
  7.9 0.0 all-gather.6.cloned.1.call-start
  7.9 1.8 copy.38
  9.7 0.0 all-gather.6.cloned.1.call-update
  9.8 0.0 all-gather.10.cloned.1.call-start
  9.8 0.7 all-gather.10.cloned.1.call-update
  10.5 0.0 all-gather.12.cloned.1.call-start
  10.5 1.1 copy.51
  11.7 0.9 fusion.22
  12.6 0.7 fusion.37
  13.2 15.7 %all-gather.8.cloned.1.call-done = bf16[512,1024]{1,0:T(8,128)(2,1)} async-done(((bf16[128,1024]{1,0:T(8,128)(2,1)}), bf16[512,1024]{1,0:T(8,128)(2,1)}) %all-gather.8.cloned.1.call-update) | async-done | bytes 1048592 | tf_op jit(solution)/shard_map/all_gather | solution.py:47
  29.0 1.5 copy.41
  30.5 17.5 %all-gather.6.cloned.1.call-done = bf16[512,1024]{0,1:T(8,128)(2,1)} async-done(((bf16[128,1024]{0,1:T(8,128)(2,1)}), bf16[512,1024]{0,1:T(8,128)(2,1)}) %all-gather.6.cloned.1.call-update) | async-done | bytes 1048592 | tf_op jit(solution)/shard_map/all_gather | solution.py:46
  48.0 2.1 fusion.42
  50.1 1.4 convolution_convert_fusion.2
  51.5 78.8 %all-gather.10.cloned.1.call-done = bf16[1024,2048]{1,0:T(8,128)(2,1)} async-done(((bf16[256,2048]{1,0:T(8,128)(2,1)}), bf16[1024,2048]{1,0:T(8,128)(2,1)}) %all-gather.10.cloned.1.call-update) | async-done | bytes 4194320 | tf_op jit(solution)/shard_map/all_gather | solution.py:65
  130.3 3.2 multiply_reduce_fusion.3
  133.5 1.8 scatter_custom_fusion
  135.3 29.0 %all_to_all.20 = bf16[4,64,2048]{2,1,0:T(8,128)(2,1)} all-to-all(bf16[4,64,2048]{2,1,0:T(8,128)(2,1)S(1)} %bitcast.80), channel_id=1, replica_groups=mesh['section'=2,'expert'=4,'dp'=4] {'expert'}, dimensions={0} | all-to-all | bytes 2097152 | tf_op jit(solution)/shard_map/all_to_all | solution.py:87
  164.3 0.0 all-gather.12.cloned.1.call-update
  164.4 0.0 all-gather.14.cloned.1.call-start
  164.4 2.2 scatter_custom_fusion.1
  166.6 28.4 %all_to_all.21 = bf16[4,64,2048]{2,1,0:T(8,128)(2,1)} all-to-all(bf16[4,64,2048]{2,1,0:T(8,128)(2,1)S(1)} %bitcast.78), channel_id=1, replica_groups=mesh['section'=2,'expert'=4,'dp'=4] {'expert'}, dimensions={0} | all-to-all | bytes 2097152 | tf_op jit(solution)/shard_map/all_to_all | solution.py:107
  195.1 0.0 all-gather.14.cloned.1.call-update
  195.1 0.0 reduce-scatter.5.cloned.1.call-start
  195.1 2.9 all-gather.12.cloned.1.call-done
  198.0 7.6 %fusion.11 = f32[1024,1024]{1,0:T(8,128)S(1)} fusion(bf16[1024,2048]{1,0:T(8,128)(2,1)} %bitcast.94, bf16[1,2048,1024]{2,1,0:T(8,128)(2,1)} %param.17), kind=kOutput, calls=%fused_computation.16 | convolution fusion | flops 4294967296 | bytes 12582912 | tf_op jit(solution)/shard_map/dot_general | solution.py:91
  205.7 6.5 %multiply_convert_fusion.2 = (bf16[1024,1024]{1,0:T(8,128)(2,1)S(1)}, f32[1024,1024]{1,0:T(8,128)}) fusion(f32[1024,1024]{1,0:T(8,128)S(1)} %fusion.11, bf16[1024,2048]{1,0:T(8,128)(2,1)S(1)} %bitcast.95, bf16[1,2048,1024]{2,1,0:T(8,128)(2,1)S(1)} %copy-done.10), kind=kOutput, calls=%fused_computation.20 | convolution fusion | flops 4301258752 | bytes 18874368 | tf_op jit(solution)/shard_map/dot_general | solution.py:92
  212.2 6.1 %fusion.14 = bf16[16,64,2048]{2,1,0:T(8,128)(2,1)} fusion(bf16[16,64,1024]{2,1,0:T(8,128)(2,1)S(1)} %bitcast.97, bf16[1,1024,2048]{2,1,0:T(8,128)(2,1)S(1)} %copy-done.9), kind=kOutput, calls=%fused_computation.24 | convolution fusion | flops 4297064448 | bytes 10485760 | tf_op jit(solution)/shard_map/dot_general | solution.py:94
  218.4 0.0 reduce-scatter.5.cloned.1.call-update
  218.4 0.2 reduce-scatter.7.cloned.1.call-start
  218.6 15.3 %all-gather.14.cloned.1.call-done = bf16[16,64,2048]{2,1,0:T(8,128)(2,1)} async-done(((bf16[4,64,2048]{2,1,0:T(8,128)(2,1)}), bf16[16,64,2048]{2,1,0:T(8,128)(2,1)}) %all-gather.14.cloned.1.call-update) | async-done | bytes 4194320 | tf_op jit(solution)/shard_map/all_gather | solution.py:108
  233.9 7.7 %fusion.3 = f32[1024,1024]{1,0:T(8,128)S(1)} fusion(bf16[1024,2048]{1,0:T(8,128)(2,1)} %bitcast.93, bf16[1,1024,2048]{2,1,0:T(8,128)(2,1)} %param.19), kind=kOutput, calls=%fused_computation.8 | convolution fusion | flops 4294967296 | bytes 12582912 | tf_op jit(solution)/shard_map/dot_general | solution.py:16
  241.7 6.9 %fusion.5 = f32[1024,2048]{1,0:T(8,128)} fusion(bf16[1,2048,1024]{2,1,0:T(8,128)(2,1)S(1)} %copy-done.11, f32[1024,1024]{1,0:T(8,128)S(1)} %fusion.3, f32[1024,1024]{1,0:T(8,128)S(1)} %copy-done.15), kind=kOutput, calls=%fused_computation.10 | convolution fusion | flops 4301258752 | bytes 20971520 | tf_op jit(solution)/shard_map/dot_general | solution.py:16
  248.5 14.3 %add_convert_fusion = bf16[1024,2048]{1,0:T(8,128)(2,1)} fusion(f32[1024,2048]{1,0:T(8,128)} %fusion.5, bf16[1,2048,1024]{2,1,0:T(8,128)(2,1)S(1)} %copy-done.12, f32[1024,1024]{1,0:T(8,128)} %copy-done.14, f32[1024,1024]{1,0:T(8,128)} %copy-done.16, f32[1024,1024]{1,0:T(8,128)} %get-tuple-element.33), kind=kOutput, calls=%fused_computation.5 | convolution fusion | flops 4309647360 | bytes 29360128 | tf_op jit(solution)/shard_map/dot_general | solution.py:16
  262.9 18.0 %reduce-scatter.5.cloned.1.call-done = bf16[4,64,2048]{2,1,0:T(8,128)(2,1)} async-done(((bf16[16,64,2048]{2,1,0:T(8,128)(2,1)}), bf16[4,64,2048]{2,1,0:T(8,128)(2,1)}) %reduce-scatter.5.cloned.1.call-update) | async-done | bytes 1048592 | tf_op jit(solution)/shard_map/reduce_scatter | solution.py:95
  280.9 4.6 all-to-all-start.1
  285.5 42.6 %reduce-scatter.7.cloned.1.call-done = bf16[4,64,2048]{2,1,0:T(8,128)(2,1)} async-done(((bf16[16,64,2048]{2,1,0:T(8,128)(2,1)}), bf16[4,64,2048]{2,1,0:T(8,128)(2,1)}) %reduce-scatter.7.cloned.1.call-update) | async-done | bytes 1048592 | tf_op jit(solution)/shard_map/reduce_scatter | solution.py:119
  328.1 4.6 all-to-all-start.3
  332.7 1.7 gather_fusion
  334.4 23.8 %all-to-all-done.3 = bf16[4,64,2048]{2,1,0:T(8,128)(2,1)S(1)} async-done(((bf16[4,64,2048]{2,1,0:T(8,128)(2,1)}), bf16[4,64,2048]{2,1,0:T(8,128)(2,1)S(1)}, u32[]{:S(2)}, u32[]{:S(2)}) %all-to-all-start.3) | async-done | bytes 1048608 | tf_op jit(solution)/shard_map/all_to_all | solution.py:125
  358.2 0.9 gather_fusion.1
  359.2 0.3 multiply_reduce_fusion.2
  359.5 2.4 add_convert_fusion.1
  361.9 3.2 convolution_convert_fusion
  365.1 0.3 reduce-scatter.9.cloned.1.call-start
  365.3 3.9 convolution_convert_fusion.3
  369.2 0.8 copy.52
  370.1 2.5 convolution_convert_fusion.1
  372.6 2.3 copy.47
  374.9 1.5 multiply_reduce_fusion
  376.4 0.4 multiply_convert_fusion.6
  376.8 0.4 multiply_convert_fusion.5
  377.2 1.3 copy.46
  378.5 2.8 pad_maximum_fusion
  381.4 0.0 all-reduce.2.cloned.1.call-start
  381.5 58.7 %reduce-scatter.11.cloned.1.call-done = bf16[256,2048]{1,0:T(8,128)(2,1)} async-done(((bf16[1024,2048]{1,0:T(8,128)(2,1)}), bf16[256,2048]{1,0:T(8,128)(2,1)}) %reduce-scatter.11.cloned.1.call-update) | async-done | bytes 1048592 | tf_op jit(solution)/shard_map/reduce_scatter | solution.py:134
  440.2 0.4 fusion.21
  440.6 0.9 copy.48
  441.5 33.5 %reduce-scatter.9.cloned.1.call-done = bf16[128,2048]{1,0:T(8,128)(2,1)} async-done(((bf16[512,2048]{1,0:T(8,128)(2,1)}), bf16[128,2048]{1,0:T(8,128)(2,1)}) %reduce-scatter.9.cloned.1.call-update) | async-done | bytes 524304 | tf_op jit(solution)/shard_map/reduce_scatter | solution.py:163
  475.0 1.9 fusion.41
  476.8 57.9 %all-reduce.2.cloned.1.call-done = bf16[256,2048]{1,0:T(8,128)(2,1)} async-done(((bf16[256,2048]{1,0:T(8,128)(2,1)}), bf16[256,2048]{1,0:T(8,128)(2,1)}) %all-reduce.2.cloned.1.call-update) | async-done | bytes 1048592 | tf_op jit(solution)/shard_map/psum | solution.py:140
  534.7 2.8 convert_element_type.123
  (43 shorter events, 0.2 us)
Async XLA Ops:
  7.2 21.8 %all-gather.8.cloned.1.call-start = ((), (), s32[]{:S(2)}) async-start(), calls=%async_computation.9 | async-start | bytes 1310720 | tf_op jit(solution)/shard_map/all_gather | solution.py:47
  7.9 40.1 %all-gather.6.cloned.1.call-start = ((), (), s32[]{:S(2)}) async-start(), calls=%async_computation.8 | async-start | bytes 1310720 | tf_op jit(solution)/shard_map/all_gather | solution.py:46
  9.8 120.6 %all-gather.10.cloned.1.call-start = ((), (), s32[]{:S(2)}) async-start(), calls=%async_computation.10 | async-start | bytes 5242880 | tf_op jit(solution)/shard_map/all_gather | solution.py:65
  10.5 187.5 %all-gather.12.cloned.1.call-start = ((), (), s32[]{:S(2)}) async-start(), calls=%async_computation.11 | async-start | bytes 5242880 | tf_op jit(solution)/shard_map/all_gather | solution.py:89
  30.5 21.0 %copy-start.6 = (bf16[512,1024]{0,1:T(8,128)(2,1)}, bf16[512,1024]{0,1:T(8,128)(2,1)S(1)}, u32[]{:S(2)}) copy-start(bf16[512,1024]{0,1:T(8,128)(2,1)S(1)} %copy.41) | copy-start | bytes 3145732
  50.1 1.4 copy-start
  51.5 82.0 %copy-start.8 = (f32[2048]{0:T(1024)S(1)}, f32[2048]{0:T(1024)}, u32[]{:S(2)}) copy-start(f32[2048]{0:T(1024)} %param.16) | copy-start | bytes 24580
  164.4 69.5 %all-gather.14.cloned.1.call-start = ((), (), s32[]{:S(2)}) async-start(), calls=%async_computation.13 | async-start | bytes 5242880 | tf_op jit(solution)/shard_map/all_gather | solution.py:108
  195.1 85.8 %reduce-scatter.5.cloned.1.call-start = ((), (), s32[]{:S(2)}) async-start(), calls=%async_computation.12 | async-start | bytes 5242880 | tf_op jit(solution)/shard_map/reduce_scatter | solution.py:95
  198.0 7.7 %copy-start.10 = (bf16[1,2048,1024]{2,1,0:T(8,128)(2,1)S(1)}, bf16[1,2048,1024]{2,1,0:T(8,128)(2,1)}, u32[]{:S(2)}) copy-start(bf16[1,2048,1024]{2,1,0:T(8,128)(2,1)} %param.18) | copy-start | bytes 12582916
  198.0 7.7 %copy-start.13 = (bf16[16,64,2048]{2,1,0:T(8,128)(2,1)S(1)}, bf16[16,64,2048]{2,1,0:T(8,128)(2,1)}, u32[]{:S(2)}) copy-start(bf16[16,64,2048]{2,1,0:T(8,128)(2,1)} %all-gather.12.cloned.1.call-done) | copy-start | bytes 12582916
  205.7 6.6 %copy-start.14 = (f32[1024,1024]{1,0:T(8,128)}, f32[1024,1024]{1,0:T(8,128)S(1)}, u32[]{:S(2)}) copy-start(f32[1024,1024]{1,0:T(8,128)S(1)} %fusion.11) | copy-start | bytes 12582916
  205.7 6.6 %copy-start.9 = (bf16[1,1024,2048]{2,1,0:T(8,128)(2,1)S(1)}, bf16[1,1024,2048]{2,1,0:T(8,128)(2,1)}, u32[]{:S(2)}) copy-start(bf16[1,1024,2048]{2,1,0:T(8,128)(2,1)} %param.19) | copy-start | bytes 12582916
  218.4 109.7 %reduce-scatter.7.cloned.1.call-start = ((), (), s32[]{:S(2)}) async-start(), calls=%async_computation.14 | async-start | bytes 5242880 | tf_op jit(solution)/shard_map/reduce_scatter | solution.py:119
  233.9 7.7 %copy-start.11 = (bf16[1,2048,1024]{2,1,0:T(8,128)(2,1)S(1)}, bf16[1,2048,1024]{2,1,0:T(8,128)(2,1)}, u32[]{:S(2)}) copy-start(bf16[1,2048,1024]{2,1,0:T(8,128)(2,1)} %param.18) | copy-start | bytes 12582916
  233.9 7.7 %copy-start.15 = (f32[1024,1024]{1,0:T(8,128)S(1)}, f32[1024,1024]{1,0:T(8,128)}, u32[]{:S(2)}) copy-start(f32[1024,1024]{1,0:T(8,128)} %copy-done.14) | copy-start | bytes 12582916
  241.7 6.9 %copy-start.16 = (f32[1024,1024]{1,0:T(8,128)}, f32[1024,1024]{1,0:T(8,128)S(1)}, u32[]{:S(2)}) copy-start(f32[1024,1024]{1,0:T(8,128)S(1)} %fusion.3) | copy-start | bytes 12582916
  241.7 6.9 %copy-start.12 = (bf16[1,2048,1024]{2,1,0:T(8,128)(2,1)S(1)}, bf16[1,2048,1024]{2,1,0:T(8,128)(2,1)}, u32[]{:S(2)}) copy-start(bf16[1,2048,1024]{2,1,0:T(8,128)(2,1)} %param.17) | copy-start | bytes 12582916
  280.9 47.2 %all-to-all-start.1 = ((bf16[4,64,2048]{2,1,0:T(8,128)(2,1)}), bf16[4,64,2048]{2,1,0:T(8,128)(2,1)S(1)}, u32[]{:S(2)}, u32[]{:S(2)}) async-start(bf16[4,64,2048]{2,1,0:T(8,128)(2,1)} %reduce-scatter.5.cloned.1.call-done), calls=%async_computation.2 | async-start | bytes 2097152 | tf_op jit(solution)/shard_map/all_to_all | solution.py:101
  328.1 30.1 %all-to-all-start.3 = ((bf16[4,64,2048]{2,1,0:T(8,128)(2,1)}), bf16[4,64,2048]{2,1,0:T(8,128)(2,1)S(1)}, u32[]{:S(2)}, u32[]{:S(2)}) async-start(bf16[4,64,2048]{2,1,0:T(8,128)(2,1)} %reduce-scatter.7.cloned.1.call-done), calls=%async_computation.5 | async-start | bytes 2097152 | tf_op jit(solution)/shard_map/all_to_all | solution.py:125
  332.7 107.5 %reduce-scatter.11.cloned.1.call-start = ((), (), s32[]{:S(2)}) async-start(), calls=%async_computation.16 | async-start | bytes 5242880 | tf_op jit(solution)/shard_map/reduce_scatter | solution.py:134
  359.2 2.7 copy-start.5
  361.9 3.5 copy-start.2
  365.0 5.0 copy-start.1
  365.1 109.9 %reduce-scatter.9.cloned.1.call-start = ((), (), s32[]{:S(2)}) async-start(), calls=%async_computation.15 | async-start | bytes 2621440 | tf_op jit(solution)/shard_map/reduce_scatter | solution.py:163
  370.1 4.8 copy-start.7
  376.8 1.8 copy-start.4
  378.5 61.6 %copy-start.3 = (bf16[512,1024]{0,1:T(8,128)(2,1)S(1)}, bf16[512,1024]{0,1:T(8,128)(2,1)}, u32[]{:S(2)}) copy-start(bf16[512,1024]{0,1:T(8,128)(2,1)} %all-gather.6.cloned.1.call-done) | copy-start | bytes 3145732
  381.4 153.3 %all-reduce.2.cloned.1.call-start = ((), (), s32[]{:S(2)}) async-start(), calls=%async_computation.17 | async-start | bytes 2097152 | tf_op jit(solution)/shard_map/psum | solution.py:140
Sparse Core Ops, SparseCore 0:
  9.5 19.4 all-gather.7
  31.1 16.8 all-gather.5
  49.5 80.7 all-gather.9
  164.5 33.4 all-gather.11
  199.4 34.4 all-gather.13
  236.3 44.5 reduce-scatter.4
  283.4 44.5 reduce-scatter.6
  365.2 74.9 reduce-scatter.10
  443.2 31.6 reduce-scatter.8
  478.0 56.6 all-reduce.1
where the time goes:
time: 545 us; the launch traced here: 544 us
  waiting for transfers between devices  366 us (67%)
  matrix products  68.7 us (13%)
  blocking collectives  57.4 us (11%)
  local copies, waits for them, and re-layouts  16.5 us (3%)
  between operations  14.4 us (3%)
  other arithmetic  11.2 us (2%)
  starting transfers between devices  9.97 us (2%)
    all_gather x1, waiting for transfers between devices, shards(): full_out = lax.all_gather(out_weight, 'expert', axis=0, tiled=True)  78.8 us
    reduce_scatter x1, waiting for transfers between devices, shards(): lax.psum_scatter(contract_first(attended, resid_grad).astype(jnp.bfloat16...  58.7 us
    psum x1, waiting for transfers between devices, shards(): weight_grad = lax.psum(grad_shard, ('section', 'dp')).astype(jnp.float32)  57.9 us
    reduce_scatter x1, waiting for transfers between devices, shards(): lax.psum_scatter(partial_grad.reshape(data_ways * experts, capacity, D).a...  42.6 us
    reduce_scatter x1, waiting for transfers between devices, shards(): lax.psum_scatter(jnp.concatenate([key_part.reshape(lax.axis_size('dp') *...  33.5 us
    dot_general x4, matrix products, contract_last(): lax.dot_general(left_side, right_side, (((1,), (1,)), ((), ())), preferre...  32.7 us
    all_to_all x1, blocking collectives, shards(): lax.all_to_all(send_buffer, 'expert', split_axis=0, concat_axis=0, tiled=...  29 us
    all_to_all x1, blocking collectives, shards(): lax.all_to_all(grad_buffer, 'expert', split_axis=0, concat_axis=0, tiled=...  28.4 us
  transfers between devices with their start and end apart: 12, of which 11 were waited for; matrix products, arithmetic and copies ran while one was open for 15% of the time, Pallas kernels for 0%

commit v1 on v0

--- a/solution.py
+++ b/solution.py
@@ -1,8 +1,10 @@
+import functools
 import math
 import jax
 import jax.numpy as jnp
 from jax import lax
 from jax.sharding import PartitionSpec as P
+from jax.lax import axis_index, axis_size, ppermute
 
 D = 2048
 HEADS = 8
@@ -10,6 +12,22 @@
 A = 1024
 FF = 4096
 epsilon = 1e-06
+
+
+def _settle_masks(a0, chip_axis):
+    n_parts = axis_size(chip_axis)
+    z1 = sorted(((i0, (i0 + 1) % n_parts) for i0 in range(n_parts)))
+    work_now = a0
+    windows = [work_now]
+    for at in range(1, n_parts):
+        work_now = ppermute(work_now, axis_name=chip_axis, perm=z1)
+        windows.insert(0, work_now)
+    small = jnp.concatenate(windows, 0)
+    ready = jnp.roll(small, (axis_index(chip_axis) + 1) * a0.shape[0], 0)
+    return ready
+
+
+report_regions_all = functools.partial(_settle_masks, chip_axis="expert")
 
 
 def contract_last(left_side, right_side):
@@ -62,7 +80,7 @@
         .reshape(tokens_here, A)
         .astype(jnp.bfloat16)
     )
-    full_out = lax.all_gather(out_weight, "expert", axis=0, tiled=True)
+    full_out = report_regions_all(out_weight)
     hidden = residual.astype(jnp.float32) + jnp.dot(
         attended, full_out, preferred_element_type=jnp.float32
     )

time: 545 us -> 507 us (0.930)
  waiting for transfers between devices: 366 us -> 319 us
  local copies, waits for them, and re-layouts: 16.5 us -> 27.5 us
    all_gather x1 -> x0, waiting for transfers between devices: 78.8 us -> none  [shards(): full_out = lax.all_gather(out_weight, 'expert', axis=0, tiled=True)]
    ppermute x0 -> x3, waiting for transfers between devices: none -> 65.7 us  [_settle_masks(): work_now = ppermute(work_now, axis_name=chip_axis, perm=z1)]
    all_gather x1, waiting for transfers between devices: 17.5 us -> 0.01 us  [shards(): lax.all_gather(attn_keys, 'dp', axis=0, tiled=True)]
    all_gather x1, waiting for transfers between devices: 15.7 us -> 0.01 us  [shards(): lax.all_gather(attn_values, 'dp', axis=0, tiled=True)]
    unnamed x36 -> x53, local copies, waits for them, and re-layouts: 2.72 us -> 12.9 us
  transfers between devices with their start and end apart: 12 -> 14, of which waited for: 11 -> 11; matrix products, arithmetic and copies ran while one was open for 15% -> 16% of each run, Pallas kernels for 0% -> 0%
where the time goes in v1:
time: 507 us; the launch traced here: 506 us
  waiting for transfers between devices  319 us (63%)
  matrix products  67.2 us (13%)
  blocking collectives  54.6 us (11%)
  local copies, waits for them, and re-layouts  27.5 us (5%)
  between operations  14.2 us (3%)
  starting transfers between devices  13.3 us (3%)
  other arithmetic  11 us (2%)
    ppermute x3, waiting for transfers between devices, _settle_masks(): work_now = ppermute(work_now, axis_name=chip_axis, perm=z1)  65.7 us
    reduce_scatter x1, waiting for transfers between devices, shards(): lax.psum_scatter(contract_first(attended, resid_grad).astype(jnp.bfloat16...  58.1 us
    psum x1, waiting for transfers between devices, shards(): weight_grad = lax.psum(grad_shard, ('section', 'dp')).astype(jnp.float32)  58.1 us
    reduce_scatter x1, waiting for transfers between devices, shards(): lax.psum_scatter(partial_grad.reshape(data_ways * experts, capacity, D).a...  42.4 us
    reduce_scatter x1, waiting for transfers between devices, shards(): lax.psum_scatter(jnp.concatenate([key_part.reshape(lax.axis_size('dp') *...  33.5 us
    dot_general x4, matrix products, contract_last(): lax.dot_general(left_side, right_side, (((1,), (1,)), ((), ())), preferre...  32.5 us
    all_to_all x1, blocking collectives, shards(): lax.all_to_all(grad_buffer, 'expert', split_axis=0, concat_axis=0, tiled=...  27.8 us
    all_to_all x1, blocking collectives, shards(): lax.all_to_all(send_buffer, 'expert', split_axis=0, concat_axis=0, tiled=...  26.9 us
  transfers between devices with their start and end apart: 14, of which 11 were waited for; matrix products, arithmetic and copies ran while one was open for 16% of the time, Pallas kernels for 0%

profile of v1, /device:TPU:0, one launch (start us, length us, event | category | flops | bytes accessed | tf_op | source)
XLA Modules:
  0.0 506.4 jit_solution(11769580457773176613)
XLA Ops:
  7.2 0.7 all-gather.7.cloned.1.call-update
  7.9 3.1 collective-permute-start
  11.1 1.8 copy.38
  12.9 23.5 %collective-permute-done = bf16[256,2048]{1,0:T(8,128)(2,1)S(1)} collective-permute-done((bf16[256,2048]{1,0:T(8,128)(2,1)}, bf16[256,2048]{1,0:T(8,128)(2,1)S(1)}, u32[]{:S(2)}, u32[]{:S(2)}) %collective-permute-start) | collective-permute-done | bytes 1048608 | tf_op jit(solution)/shard_map/ppermute | solution.py:23
  36.5 1.1 copy.51
  37.6 25.1 %collective-permute-done.1 = bf16[256,2048]{1,0:T(8,128)(2,1)} collective-permute-done((bf16[256,2048]{1,0:T(8,128)(2,1)S(1)}, bf16[256,2048]{1,0:T(8,128)(2,1)}, u32[]{:S(2)}, u32[]{:S(2)}) %collective-permute-start.1) | collective-permute-done | bytes 1048608 | tf_op jit(solution)/shard_map/ppermute | solution.py:23
  62.7 0.9 fusion.32
  63.6 0.7 fusion.47
  64.2 2.3 copy.41
  66.5 2.1 fusion.54
  68.7 2.5 convolution_convert_fusion.2
  71.2 17.0 %collective-permute-done.2 = bf16[256,2048]{1,0:T(8,128)(2,1)} collective-permute-done((bf16[256,2048]{1,0:T(8,128)(2,1)}, bf16[256,2048]{1,0:T(8,128)(2,1)}, u32[]{:S(2)}, u32[]{:S(2)}) %collective-permute-start.2) | collective-permute-done | bytes 1048608 | tf_op jit(solution)/shard_map/ppermute | solution.py:23
  88.3 1.3 constant_dynamic-update-slice_fusion.7
  89.6 1.3 constant_dynamic-update-slice_fusion.6
  90.8 0.1 constant_dynamic-update-slice_fusion.5
  90.9 0.1 constant_dynamic-update-slice_fusion.4
  91.0 1.4 constant_dynamic-update-slice_fusion.3
  92.4 1.3 constant_dynamic-update-slice_fusion.2
  93.7 0.1 constant_dynamic-update-slice_fusion.1
  93.9 3.2 copy-done
  97.1 0.8 multiply_reduce_fusion.3
  98.0 1.8 scatter_custom_fusion
  99.7 26.9 %all_to_all.20 = bf16[4,64,2048]{2,1,0:T(8,128)(2,1)} all-to-all(bf16[4,64,2048]{2,1,0:T(8,128)(2,1)S(1)} %bitcast.78), channel_id=1, replica_groups=mesh['section'=2,'expert'=4,'dp'=4] {'expert'}, dimensions={0} | all-to-all | bytes 2097152 | tf_op jit(solution)/shard_map/all_to_all | solution.py:105
  126.7 2.2 scatter_custom_fusion.1
  128.9 27.8 %all_to_all.21 = bf16[4,64,2048]{2,1,0:T(8,128)(2,1)} all-to-all(bf16[4,64,2048]{2,1,0:T(8,128)(2,1)S(1)} %bitcast.76), channel_id=1, replica_groups=mesh['section'=2,'expert'=4,'dp'=4] {'expert'}, dimensions={0} | all-to-all | bytes 2097152 | tf_op jit(solution)/shard_map/all_to_all | solution.py:125
  156.7 0.2 reduce-scatter.5.cloned.1.call-start
  156.9 2.8 all-gather.9.cloned.1.call-done
  159.7 7.6 %fusion.11 = f32[1024,1024]{1,0:T(8,128)S(1)} fusion(bf16[1024,2048]{1,0:T(8,128)(2,1)} %bitcast.92, bf16[1,2048,1024]{2,1,0:T(8,128)(2,1)} %param.17), kind=kOutput, calls=%fused_computation.16 | convolution fusion | flops 4294967296 | bytes 12582912 | tf_op jit(solution)/shard_map/dot_general | solution.py:109
  167.4 6.5 %multiply_convert_fusion.2 = (bf16[1024,1024]{1,0:T(8,128)(2,1)S(1)}, f32[1024,1024]{1,0:T(8,128)}) fusion(f32[1024,1024]{1,0:T(8,128)S(1)} %fusion.11, bf16[1024,2048]{1,0:T(8,128)(2,1)S(1)} %bitcast.93, bf16[1,2048,1024]{2,1,0:T(8,128)(2,1)S(1)} %copy-done.15), kind=kOutput, calls=%fused_computation.20 | convolution fusion | flops 4301258752 | bytes 18874368 | tf_op jit(solution)/shard_map/dot_general | solution.py:110
  173.9 6.1 %fusion.14 = bf16[16,64,2048]{2,1,0:T(8,128)(2,1)} fusion(bf16[16,64,1024]{2,1,0:T(8,128)(2,1)S(1)} %bitcast.95, bf16[1,1024,2048]{2,1,0:T(8,128)(2,1)S(1)} %copy-done.14), kind=kOutput, calls=%fused_computation.24 | convolution fusion | flops 4297064448 | bytes 10485760 | tf_op jit(solution)/shard_map/dot_general | solution.py:112
  180.1 0.3 reduce-scatter.7.cloned.1.call-start
  180.3 15.3 %all-gather.11.cloned.1.call-done = bf16[16,64,2048]{2,1,0:T(8,128)(2,1)} async-done(((bf16[4,64,2048]{2,1,0:T(8,128)(2,1)}), bf16[16,64,2048]{2,1,0:T(8,128)(2,1)}) %all-gather.11.cloned.1.call-update) | async-done | bytes 4194320 | tf_op jit(solution)/shard_map/all_gather | solution.py:126
  195.6 7.7 %fusion.3 = f32[1024,1024]{1,0:T(8,128)S(1)} fusion(bf16[1024,2048]{1,0:T(8,128)(2,1)} %bitcast.91, bf16[1,1024,2048]{2,1,0:T(8,128)(2,1)} %param.19), kind=kOutput, calls=%fused_computation.8 | convolution fusion | flops 4294967296 | bytes 12582912 | tf_op jit(solution)/shard_map/dot_general | solution.py:34
  203.4 6.7 %fusion.5 = f32[1024,2048]{1,0:T(8,128)} fusion(bf16[1,2048,1024]{2,1,0:T(8,128)(2,1)S(1)} %copy-done.16, f32[1024,1024]{1,0:T(8,128)S(1)} %fusion.3, f32[1024,1024]{1,0:T(8,128)S(1)} %copy-done.20), kind=kOutput, calls=%fused_computation.10 | convolution fusion | flops 4301258752 | bytes 20971520 | tf_op jit(solution)/shard_map/dot_general | solution.py:34
  210.1 14.3 %add_convert_fusion = bf16[1024,2048]{1,0:T(8,128)(2,1)} fusion(f32[1024,2048]{1,0:T(8,128)} %fusion.5, bf16[1,2048,1024]{2,1,0:T(8,128)(2,1)S(1)} %copy-done.17, f32[1024,1024]{1,0:T(8,128)} %copy-done.19, f32[1024,1024]{1,0:T(8,128)} %copy-done.21, f32[1024,1024]{1,0:T(8,128)} %get-tuple-element.33), kind=kOutput, calls=%fused_computation.5 | convolution fusion | flops 4309647360 | bytes 29360128 | tf_op jit(solution)/shard_map/dot_general | solution.py:34
  224.5 18.1 %reduce-scatter.5.cloned.1.call-done = bf16[4,64,2048]{2,1,0:T(8,128)(2,1)} async-done(((bf16[16,64,2048]{2,1,0:T(8,128)(2,1)}), bf16[4,64,2048]{2,1,0:T(8,128)(2,1)}) %reduce-scatter.5.cloned.1.call-update) | async-done | bytes 1048592 | tf_op jit(solution)/shard_map/reduce_scatter | solution.py:113
  242.6 4.6 all-to-all-start.1
  247.2 42.4 %reduce-scatter.7.cloned.1.call-done = bf16[4,64,2048]{2,1,0:T(8,128)(2,1)} async-done(((bf16[16,64,2048]{2,1,0:T(8,128)(2,1)}), bf16[4,64,2048]{2,1,0:T(8,128)(2,1)}) %reduce-scatter.7.cloned.1.call-update) | async-done | bytes 1048592 | tf_op jit(solution)/shard_map/reduce_scatter | solution.py:137
  289.6 4.6 all-to-all-start.3
  294.2 1.7 gather_fusion
  296.0 23.8 %all-to-all-done.3 = bf16[4,64,2048]{2,1,0:T(8,128)(2,1)S(1)} async-done(((bf16[4,64,2048]{2,1,0:T(8,128)(2,1)}), bf16[4,64,2048]{2,1,0:T(8,128)(2,1)S(1)}, u32[]{:S(2)}, u32[]{:S(2)}) %all-to-all-start.3) | async-done | bytes 1048608 | tf_op jit(solution)/shard_map/all_to_all | solution.py:143
  319.8 0.9 gather_fusion.1
  320.7 0.3 multiply_reduce_fusion.2
  321.0 2.2 add_convert_fusion.1
  323.3 0.8 copy-done.3
  324.1 3.2 convolution_convert_fusion
  327.3 0.3 reduce-scatter.9.cloned.1.call-start
  327.6 0.7 copy-done.4
  328.3 3.7 fusion.29
  332.0 0.8 copy.52
  332.9 2.5 convolution_convert_fusion.1
  335.4 2.3 copy.47
  337.7 1.5 multiply_reduce_fusion
  339.2 0.4 multiply_convert_fusion.6
  339.6 0.4 multiply_convert_fusion.5
  340.0 1.3 copy.46
  341.4 2.8 pad_maximum_fusion
  344.2 58.1 %reduce-scatter.11.cloned.1.call-done = bf16[256,2048]{1,0:T(8,128)(2,1)} async-done(((bf16[1024,2048]{1,0:T(8,128)(2,1)}), bf16[256,2048]{1,0:T(8,128)(2,1)}) %reduce-scatter.11.cloned.1.call-update) | async-done | bytes 1048592 | tf_op jit(solution)/shard_map/reduce_scatter | solution.py:152
  402.4 0.4 fusion.28
  402.9 0.8 copy.48
  403.7 33.5 %reduce-scatter.9.cloned.1.call-done = bf16[128,2048]{1,0:T(8,128)(2,1)} async-done(((bf16[512,2048]{1,0:T(8,128)(2,1)}), bf16[128,2048]{1,0:T(8,128)(2,1)}) %reduce-scatter.9.cloned.1.call-update) | async-done | bytes 524304 | tf_op jit(solution)/shard_map/reduce_scatter | solution.py:181
  437.2 1.9 fusion.53
  439.0 58.1 %all-reduce.2.cloned.1.call-done = bf16[256,2048]{1,0:T(8,128)(2,1)} async-done(((bf16[256,2048]{1,0:T(8,128)(2,1)}), bf16[256,2048]{1,0:T(8,128)(2,1)}) %all-reduce.2.cloned.1.call-update) | async-done | bytes 1048592 | tf_op jit(solution)/shard_map/psum | solution.py:158
  497.1 2.8 convert_element_type.123
  (64 shorter events, 0.5 us)
Async XLA Ops:
  7.2 57.1 %all-gather.7.cloned.1.call-start = ((), (), s32[]{:S(2)}) async-start(), calls=%async_computation.9 | async-start | bytes 1310720 | tf_op jit(solution)/shard_map/all_gather | solution.py:65
  7.9 58.6 %all-gather.5.cloned.1.call-start = ((), (), s32[]{:S(2)}) async-start(), calls=%async_computation.8 | async-start | bytes 1310720 | tf_op jit(solution)/shard_map/all_gather | solution.py:64
  7.9 28.5 %collective-permute-start = (bf16[256,2048]{1,0:T(8,128)(2,1)}, bf16[256,2048]{1,0:T(8,128)(2,1)S(1)}, u32[]{:S(2)}, u32[]{:S(2)}) collective-permute-start(bf16[256,2048]{1,0:T(8,128)(2,1)} %param.15), channel_id=1, source_target_pairs={{0,4},{4,8},{8,12},{12,0},{1,5},{5,9},{9,13},{13,1},{2,6},{6,10},{... | collective-permute-start | bytes 3145736 | tf_op jit(solution)/shard_map/ppermute | solution.py:23
  12.9 146.8 %all-gather.9.cloned.1.call-start = ((), (), s32[]{:S(2)}) async-start(), calls=%async_computation.10 | async-start | bytes 5242880 | tf_op jit(solution)/shard_map/all_gather | solution.py:107
  36.4 26.2 %collective-permute-start.1 = (bf16[256,2048]{1,0:T(8,128)(2,1)S(1)}, bf16[256,2048]{1,0:T(8,128)(2,1)}, u32[]{:S(2)}, u32[]{:S(2)}) collective-permute-start(bf16[256,2048]{1,0:T(8,128)(2,1)S(1)} %collective-permute-done), channel_id=1, source_target_pairs={{0,4},{4,8},{8,12},{12,0},{1,5},{5,9},{9,13},{13,1},{2,6},{6,10},{... | collective-permute-start | bytes 3145736 | tf_op jit(solution)/shard_map/ppermute | solution.py:23
  62.7 25.6 %collective-permute-start.2 = (bf16[256,2048]{1,0:T(8,128)(2,1)}, bf16[256,2048]{1,0:T(8,128)(2,1)}, u32[]{:S(2)}, u32[]{:S(2)}) collective-permute-start(bf16[256,2048]{1,0:T(8,128)(2,1)} %collective-permute-done.1), channel_id=1, source_target_pairs={{0,4},{4,8},{8,12},{12,0},{1,5},{5,9},{9,13},{13,1},{2,6},{6,10},{... | collective-permute-start | bytes 3145736 | tf_op jit(solution)/shard_map/ppermute | solution.py:23
  68.7 2.5 copy-start.1
  71.2 22.7 %copy-start.9 = (bf16[8,128,128]{1,2,0:T(8,128)(2,1)}, bf16[8,128,128]{1,2,0:T(8,128)(2,1)S(1)}, u32[]{:S(2)}) copy-start(bf16[8,128,128]{1,2,0:T(8,128)(2,1)S(1)} %convolution_convert_fusion.2) | copy-start | bytes 786436
  71.2 19.7 %copy-start.5 = (bf16[256,2048]{1,0:T(8,128)(2,1)S(1)}, bf16[256,2048]{1,0:T(8,128)(2,1)}, u32[]{:S(2)}) copy-start(bf16[256,2048]{1,0:T(8,128)(2,1)} %param.15) | copy-start | bytes 3145732
  91.0 6.1 %copy-start.12 = (bf16[128,2048]{1,0:T(8,128)(2,1)S(1)}, bf16[128,2048]{1,0:T(8,128)(2,1)}, u32[]{:S(2)}) copy-start(bf16[128,2048]{1,0:T(8,128)(2,1)} %param.11) | copy-start | bytes 1572868
  93.8 4.2 copy-start.13
  93.8 3.3 copy-start
  126.6 69.0 %all-gather.11.cloned.1.call-start = ((), (), s32[]{:S(2)}) async-start(), calls=%async_computation.12 | async-start | bytes 5242880 | tf_op jit(solution)/shard_map/all_gather | solution.py:126
  156.7 85.9 %reduce-scatter.5.cloned.1.call-start = ((), (), s32[]{:S(2)}) async-start(), calls=%async_computation.11 | async-start | bytes 5242880 | tf_op jit(solution)/shard_map/reduce_scatter | solution.py:113
  159.7 7.7 %copy-start.15 = (bf16[1,2048,1024]{2,1,0:T(8,128)(2,1)S(1)}, bf16[1,2048,1024]{2,1,0:T(8,128)(2,1)}, u32[]{:S(2)}) copy-start(bf16[1,2048,1024]{2,1,0:T(8,128)(2,1)} %param.18) | copy-start | bytes 12582916
  159.7 7.7 %copy-start.18 = (bf16[16,64,2048]{2,1,0:T(8,128)(2,1)S(1)}, bf16[16,64,2048]{2,1,0:T(8,128)(2,1)}, u32[]{:S(2)}) copy-start(bf16[16,64,2048]{2,1,0:T(8,128)(2,1)} %all-gather.9.cloned.1.call-done) | copy-start | bytes 12582916
  167.4 6.5 %copy-start.19 = (f32[1024,1024]{1,0:T(8,128)}, f32[1024,1024]{1,0:T(8,128)S(1)}, u32[]{:S(2)}) copy-start(f32[1024,1024]{1,0:T(8,128)S(1)} %fusion.11) | copy-start | bytes 12582916
  167.4 6.5 %copy-start.14 = (bf16[1,1024,2048]{2,1,0:T(8,128)(2,1)S(1)}, bf16[1,1024,2048]{2,1,0:T(8,128)(2,1)}, u32[]{:S(2)}) copy-start(bf16[1,1024,2048]{2,1,0:T(8,128)(2,1)} %param.19) | copy-start | bytes 12582916
  180.1 109.5 %reduce-scatter.7.cloned.1.call-start = ((), (), s32[]{:S(2)}) async-start(), calls=%async_computation.13 | async-start | bytes 5242880 | tf_op jit(solution)/shard_map/reduce_scatter | solution.py:137
  195.6 7.7 %copy-start.16 = (bf16[1,2048,1024]{2,1,0:T(8,128)(2,1)S(1)}, bf16[1,2048,1024]{2,1,0:T(8,128)(2,1)}, u32[]{:S(2)}) copy-start(bf16[1,2048,1024]{2,1,0:T(8,128)(2,1)} %param.18) | copy-start | bytes 12582916
  195.6 7.7 %copy-start.20 = (f32[1024,1024]{1,0:T(8,128)S(1)}, f32[1024,1024]{1,0:T(8,128)}, u32[]{:S(2)}) copy-start(f32[1024,1024]{1,0:T(8,128)} %copy-done.19) | copy-start | bytes 12582916
  203.4 6.7 %copy-start.21 = (f32[1024,1024]{1,0:T(8,128)}, f32[1024,1024]{1,0:T(8,128)S(1)}, u32[]{:S(2)}) copy-start(f32[1024,1024]{1,0:T(8,128)S(1)} %fusion.3) | copy-start | bytes 12582916
  203.4 6.7 %copy-start.17 = (bf16[1,2048,1024]{2,1,0:T(8,128)(2,1)S(1)}, bf16[1,2048,1024]{2,1,0:T(8,128)(2,1)}, u32[]{:S(2)}) copy-start(bf16[1,2048,1024]{2,1,0:T(8,128)(2,1)} %param.17) | copy-start | bytes 12582916
  242.6 47.0 %all-to-all-start.1 = ((bf16[4,64,2048]{2,1,0:T(8,128)(2,1)}), bf16[4,64,2048]{2,1,0:T(8,128)(2,1)S(1)}, u32[]{:S(2)}, u32[]{:S(2)}) async-start(bf16[4,64,2048]{2,1,0:T(8,128)(2,1)} %reduce-scatter.5.cloned.1.call-done), calls=%async_computation.2 | async-start | bytes 2097152 | tf_op jit(solution)/shard_map/all_to_all | solution.py:119
  289.6 30.2 %all-to-all-start.3 = ((bf16[4,64,2048]{2,1,0:T(8,128)(2,1)}), bf16[4,64,2048]{2,1,0:T(8,128)(2,1)S(1)}, u32[]{:S(2)}, u32[]{:S(2)}) async-start(bf16[4,64,2048]{2,1,0:T(8,128)(2,1)} %reduce-scatter.7.cloned.1.call-done), calls=%async_computation.5 | async-start | bytes 2097152 | tf_op jit(solution)/shard_map/all_to_all | solution.py:143
  294.2 108.1 %reduce-scatter.11.cloned.1.call-start = ((), (), s32[]{:S(2)}) async-start(), calls=%async_computation.15 | async-start | bytes 5242880 | tf_op jit(solution)/shard_map/reduce_scatter | solution.py:152
  296.0 25.0 %copy-start.8 = (bf16[128,2048]{1,0:T(8,128)(2,1)S(1)}, bf16[128,2048]{1,0:T(8,128)(2,1)}, u32[]{:S(2)}) copy-start(bf16[128,2048]{1,0:T(8,128)(2,1)} %gather_fusion) | copy-start | bytes 1572868
  320.7 3.3 copy-start.10
  323.3 0.8 copy-start.3
  327.3 1.0 copy-start.4
  327.3 5.6 %copy-start.2 = (f32[8,128,512]{2,1,0:T(8,128)S(1)}, f32[8,128,512]{2,1,0:T(8,128)}, u32[]{:S(2)}) copy-start(f32[8,128,512]{2,1,0:T(8,128)} %copy-done.1) | copy-start | bytes 6291460
  327.3 109.9 %reduce-scatter.9.cloned.1.call-start = ((), (), s32[]{:S(2)}) async-start(), calls=%async_computation.14 | async-start | bytes 2621440 | tf_op jit(solution)/shard_map/reduce_scatter | solution.py:181
  332.9 4.8 copy-start.11
  339.6 1.8 copy-start.7
  341.4 61.1 %copy-start.6 = (bf16[512,1024]{0,1:T(8,128)(2,1)S(1)}, bf16[512,1024]{0,1:T(8,128)(2,1)}, u32[]{:S(2)}) copy-start(bf16[512,1024]{0,1:T(8,128)(2,1)} %all-gather.5.cloned.1.call-done) | copy-start | bytes 3145732
  344.2 152.9 %all-reduce.2.cloned.1.call-start = ((), (), s32[]{:S(2)}) async-start(), calls=%async_computation.16 | async-start | bytes 2097152 | tf_op jit(solution)/shard_map/psum | solution.py:158
Sparse Core Ops, SparseCore 0:
  9.5 19.4 all-gather.6
  31.1 16.8 all-gather.4
  126.8 32.9 all-gather.8
  161.1 34.4 all-gather.10
  198.0 44.5 reduce-scatter.4
  245.0 44.5 reduce-scatter.6
  327.4 74.9 reduce-scatter.10
  405.5 31.6 reduce-scatter.8
  440.3 56.7 all-reduce.1
